TPU v7x, 32 devices: a whole 2x2x4 slice. The times are simulated.
32 devices in a mesh: tm: 32 (over z, y, x, core).
Axes of the slice: x: 2, y: 2, z: 4, core: 2. Of those that a mesh axis runs over, the one named last changes fastest.
Arguments:
- initial: float32 [2, 64, 64], replicated, may hold values from 0 to 0.6
- coarse_guess: float32 [32, 2, 64, 64], P('tm'), may hold values from 0 to 0.6
- feed_rate: float32 [64, 64], replicated, may hold values from 0.02 to 0.08
- kill_rate: float32 [64, 64], replicated, may hold values from 0.03 to 0.07
Outputs:
- trajectory: float32 [128, 2, 64, 64], P('tm')
- c_residual: float32 [32, 2, 64, 64], P('tm')
- group_coarse: float32 [32, 2, 64, 64], P('tm')
- level_defect: float32 [32, 2, 64, 64], P('tm')
All inputs are finite; a program needn't handle non-finite values.
Results may differ from a plain program's by a relative error of at most 0.0004.
Values sent between devices are 32-bit elements; how exact they have to be, the bound alone decides.
A program may use at most 64 MiB of HBM per device.

v0:
```python
import functools

import jax
import jax.numpy as jnp
import ml_dtypes
import numpy as np
from jax import lax
from jax.experimental import pallas as pl
from jax.experimental.pallas import tpu as pltpu
from jax.sharding import PartitionSpec as P

STEPS_DEV = 4
GROUP = 16
INPUTS = 10
LEADERS = 4
PIECES = STEPS_DEV + 3
VMEM_GRANT = 16 * 2**20

diffusion = (0.2, 0.1)
interval_time = 0.03125
MESH = pl.DeviceIdType.MESH
single = np.float32


def cosine_basis(length):
    positions = np.arange(length, dtype=single)
    angles = single(np.pi) * (positions[:, None] + single(0.5)) * positions[None, :] / single(length)
    weight = np.where(positions == 0, np.sqrt(single(1.0 / length)), np.sqrt(single(2.0 / length)))
    return (np.cos(angles) * weight[None, :].astype(single)).astype(single)


def eigen_values(length):
    positions = np.arange(length, dtype=single)
    waves = np.sin(single(np.pi) * positions / single(2.0 * length))
    return (single(-4.0) * waves * waves).astype(single)


def halves(matrix):
    high = matrix.astype(ml_dtypes.bfloat16)
    low = (matrix - high.astype(np.float64)).astype(ml_dtypes.bfloat16)
    return high, low


def factors(rows, cols, time_step, rate, rank):
    basis_rows = cosine_basis(rows).astype(np.float64)
    basis_cols = cosine_basis(cols).astype(np.float64)
    spectrum = eigen_values(rows).astype(np.float64)[:, None] + eigen_values(cols).astype(np.float64)[None, :]
    factor = 1.0 / (1.0 - time_step * rate * spectrum)
    left, sizes, right = np.linalg.svd(factor)
    if rank is None:
        rank = 1
        while np.abs(factor - (left[:, :rank] * sizes[:rank]) @ right[:rank]).max() > 2.0**-26:
            rank += 1
        return rank
    left = left[:, :rank] * np.sqrt(sizes[:rank])
    right = right[:rank].T * np.sqrt(sizes[:rank])
    scale = left[0, 0]
    left[:, 0] /= scale
    right[:, 0] *= scale
    firsts = [basis_rows @ np.diag(left[:, k]) @ basis_rows.T for k in range(rank)]
    seconds = [basis_cols @ np.diag(right[:, k]) @ basis_cols.T for k in range(rank)]
    firsts[0] = firsts[0] - np.eye(rows)
    seconds[0] = seconds[0] - np.eye(cols)
    return firsts, seconds


@functools.lru_cache(maxsize=None)
def solve_tables(rows, cols, time_step):
    rank = max(factors(rows, cols, time_step, rate, None) for rate in diffusion)
    rank = max(rank, 2)
    species = [factors(rows, cols, time_step, rate, rank) for rate in diffusion]
    short = rank == 2
    rights, lefts = [], []
    for firsts, seconds in species:
        highs, lows = [], []
        for second in seconds:
            high, low = halves(second)
            highs += [high] * 2
            lows += [low] * 2
        high = np.concatenate(highs, 1)
        low = np.concatenate(lows, 1)
        rights.append(np.concatenate([high, high, low], 0))
        pairs = [halves(first) for first in firsts]
        highs = [high for high, low in pairs]
        lows = [low for high, low in pairs]
        if short:
            lefts.append(np.concatenate(highs + highs[:1] + lows[:1], 1))
        else:
            lefts.append(np.concatenate(highs + highs + lows, 1))
    return np.stack(rights), np.stack(lefts)


def kernel(devices, sizes, *refs):
    sources = refs[:INPUTS]
    packed_ref = refs[INPUTS]
    held = refs[INPUTS + 1 : 2 * INPUTS + 1]
    (initial_ref, guess_ref, feed_ref, kill_ref) = held[:4]
    table_refs = (held[4:6], held[6:8], held[8:10])
    (rates, b_buf, s_buf, r_buf, p_buf, e_buf, u_buf, prior_buf, end_buf, mine_buf, b_out, r_out, p_out, zero_buf, own_buf, tail_buf) = refs[
        2 * INPUTS + 1 : 2 * INPUTS + 17
    ]
    (
        send_b, recv_b, send_s, recv_s, send_e, recv_e, send_u, send_w,
        recv_u, recv_v, recv_w, send_r, recv_r, send_p, recv_p, load, send_own, recv_own,
    ) = refs[2 * INPUTS + 17 :]
    rows, cols = sizes
    groups = devices // GROUP
    half = GROUP // 2
    me = lax.axis_index("tm")
    group = me // GROUP
    member = me % GROUP
    base = group * GROUP
    slot = (member + 2) % GROUP
    opens = group == 0
    wraps = member >= GROUP - 2
    forwards = jnp.logical_and(wraps, group < groups - 1)
    leads = jnp.logical_and(member >= half, member % 2 == 1)
    relaxes = member == jnp.where(opens, 0, half - 1)
    corrects = jnp.logical_and(relaxes, group > 0)
    serves = jnp.logical_and(leads, jnp.logical_or(opens, member < GROUP - 1))
    listeners = (LEADERS + 1) * (groups - 1 - group)

    loads = [pltpu.make_async_copy(source, target, load.at[i]) for i, (source, target) in enumerate(zip(sources, held))]
    for i in (4, 5, 1, 2, 3, 0, 6, 7, 8, 9):
        loads[i].start()

    def leader(i):
        return GROUP - 1 - 2 * i

    barrier = pltpu.get_barrier_semaphore()

    def greet(other):
        pl.semaphore_signal(barrier, inc=1, device_id=(other,), device_id_type=MESH)

    def greet_peer(i, carry):
        greet(base + (member + 1 + i) % GROUP)
        return carry

    def relaxer(other):
        return other * GROUP + jnp.where(other == 0, 0, half - 1)

    def greet_relaxer(other, carry):
        greet(relaxer(other))
        return carry

    @pl.when(jnp.logical_or(leads, relaxes))
    def _():
        lax.fori_loop(0, group, greet_relaxer, 0)

    @pl.when(jnp.logical_and(jnp.logical_or(leads, relaxes), group > 0))
    def _():
        greet(base - 2)
        greet(base - 1)

    @pl.when(jnp.logical_and(group > 0, member <= 1))
    def _():
        greet(me - 2)

    @pl.when(jnp.logical_and(group > 0, member == 0))
    def _():
        greet(me - 1)

    lax.fori_loop(0, GROUP - 1, greet_peer, 0)

    def await_barrier():
        crossing = jnp.where(forwards, LEADERS + member - (GROUP - 4), 0)
        pl.semaphore_wait(barrier, GROUP - 1 + crossing + jnp.where(relaxes, listeners, 0))

    def remote(source, target, send, recv, other):
        return pltpu.make_async_remote_copy(
            src_ref=source, dst_ref=target, send_sem=send, recv_sem=recv,
            device_id=(other,), device_id_type=MESH,
        )

    left_half = lax.broadcasted_iota(jnp.int32, (rows, 2 * cols), 1) < cols
    fine_step = interval_time / STEPS_DEV
    steps = (fine_step, interval_time, interval_time * GROUP)
    for copy in loads[:6]:
        copy.wait()
    feed = jnp.concatenate([feed_ref[...]] * 2, axis=1)
    kill = jnp.concatenate([kill_ref[...]] * 2, axis=1)
    for level, step in enumerate(steps):
        rates[3 * level] = 1.0 - step * feed
        rates[3 * level + 1] = step * feed
        rates[3 * level + 2] = 1.0 - step * (feed + kill)

    def double(value):
        return jnp.concatenate([value, value], axis=1)

    def join(state):
        return jnp.where(left_half, state[0], state[1])

    def spread(value):
        turned = pltpu.roll(value, cols, 1)
        return jnp.where(left_half, value, turned), jnp.where(left_half, turned, value)

    def plus(state, other):
        return state[0] + other[0], state[1] + other[1]

    def minus(state, other):
        return state[0] - other[0], state[1] - other[1]

    def split(value):
        high = value.astype(jnp.bfloat16)
        low = (value - high.astype(jnp.float32)).astype(jnp.bfloat16)
        return high, low

    def dot(first, second):
        return jnp.dot(first, second, preferred_element_type=jnp.float32)

    def stacked_rows(values):
        return jnp.concatenate(values, 0) if len(values) > 1 else values[0]

    def spectral(level, kind, main):
        count = main.shape[0] // rows
        high = main.astype(jnp.bfloat16)
        wide = high.astype(jnp.float32)
        mixed = jnp.where(stacked_rows([left_half] * count), wide, main - wide).astype(jnp.bfloat16)
        return dot(jnp.concatenate([mixed, high[:, :cols]], 1), table_refs[level][0][kind])

    def gather_terms(main, product):
        count = main.shape[0] // rows
        terms = product.shape[1] // (2 * cols)
        parts = [product[:, 2 * cols * k : 2 * cols * (k + 1)] for k in range(terms)]
        first = main + parts[0]
        parts[0] = first
        columns = []
        for n in range(count):
            pieces = [part[rows * n : rows * (n + 1)] for part in parts]
            if terms == 2:
                first_high, first_low = split(pieces[0])
                stack = [first_high, pieces[1].astype(jnp.bfloat16), first_low, first_high]
            else:
                pairs = [split(piece) for piece in pieces]
                stack = [a for a, b in pairs] + [b for a, b in pairs] + [a for a, b in pairs]
            columns.append(jnp.concatenate(stack, 0))
        return first, jnp.concatenate(columns, 1) if count > 1 else columns[0]

    def react(level, states):
        step = steps[level]
        reacted = ([], [])
        for substrate, catalyst in states:
            uptake = step * (substrate * (catalyst * catalyst))
            reacted[0].append(rates[3 * level] * substrate + rates[3 * level + 1] - uptake)
            reacted[1].append(rates[3 * level + 2] * catalyst + uptake)
        return [stacked_rows(values) for values in reacted]

    def evolve_all(*items):
        mains = [(level, kind, main) for level, states in items for kind, main in enumerate(react(level, states))]
        products = [spectral(level, kind, main) for level, kind, main in mains]
        gathered = [gather_terms(main, product) for (_, _, main), product in zip(mains, products)]
        smalls = [dot(table_refs[level][1][kind], stack) for (level, kind, _), (_, stack) in zip(mains, gathered)]
        solved = [
            [first[rows * n : rows * (n + 1)] + small[:, 2 * cols * n : 2 * cols * (n + 1)] for n in range(first.shape[0] // rows)]
            for (first, stack), small in zip(gathered, smalls)
        ]
        return [list(zip(*solved[2 * i : 2 * i + 2])) for i in range(len(items))]

    def evolve(level, *states):
        return evolve_all((level, states))[0]

    start = double(initial_ref[0]), double(initial_ref[1])
    own = double(guess_ref[0, 0]), double(guess_ref[0, 1])

    def fine_turn(unused, states):
        return tuple(evolve(0, *states))

    def prepare(*states):
        relaxed = lax.fori_loop(0, STEPS_DEV, fine_turn, states, unroll=True)
        r_out[...] = join(relaxed[0])
        for copy in loads[6:]:
            copy.wait()
        arrived, (image,) = evolve_all((0, relaxed), (1, relaxed[:1]))
        arrived = lax.fori_loop(1, STEPS_DEV, fine_turn, tuple(arrived), unroll=True)
        p_out[...] = join(arrived[0])
        b_out[...] = join(minus(arrived[0], image))
        if len(states) > 1:
            zero_buf[0] = join(relaxed[1])
            zero_buf[1] = join(arrived[1])

    pairs = jnp.logical_and(opens, jnp.logical_or(member >= half, member <= 1))

    @pl.when(pairs)
    def _():
        prepare(own, start)

    @pl.when(jnp.logical_not(pairs))
    def _():
        prepare(own)

    r_copy = remote(r_out, r_buf, send_r, recv_r, me + 1)
    p_copy = remote(p_out, p_buf, send_p, recv_p, me + 2)
    reach = base + jnp.where(wraps, GROUP, 0)

    def b_copy(i, other):
        return remote(b_out, b_buf.at[slot], send_b.at[i], recv_b.at[slot], other)

    reached_relaxer = relaxer(group + jnp.where(wraps, 1, 0))
    s_copy = remote(r_out, s_buf, send_s, recv_s, reached_relaxer)

    sends = jnp.logical_or(forwards, jnp.logical_not(wraps))
    defers = jnp.logical_and(opens, jnp.logical_and(member >= half + LEADERS, jnp.logical_not(wraps)))

    def over_relaxer(act):
        @pl.when(jnp.logical_and(forwards, member == GROUP - 2))
        def _():
            act(s_copy)

        @pl.when(jnp.logical_and(sends, me != reached_relaxer))
        def _():
            act(b_copy(LEADERS, reached_relaxer))

    def over_leaders(act, where):
        for i in range(LEADERS):

            @pl.when(jnp.logical_and(jnp.logical_and(sends, where), slot <= leader(i)))
            def _():
                act(b_copy(i, reach + leader(i)))

    await_barrier()

    @pl.when(jnp.logical_not(defers))
    def _():
        over_relaxer(lambda copy: copy.start())

    over_leaders(lambda copy: copy.start(), me >= 0)

    @pl.when(defers)
    def _():
        over_leaders(lambda copy: copy.wait_send(), me >= 0)
        over_relaxer(lambda copy: copy.start())

    @pl.when(me + 2 < devices)
    def _():
        p_copy.start()

    @pl.when(me + 1 < devices)
    def _():
        r_copy.start()

    @pl.when(relaxes)
    def _():
        pltpu.make_async_copy(b_out, b_buf.at[slot], recv_b.at[slot]).start()

    @pl.when(me == 0)
    def _():
        r_buf[...] = zero_buf[0]
        p_buf[...] = zero_buf[0]

    @pl.when(me == 1)
    def _():
        p_buf[...] = zero_buf[1]

    below = member - half - 1
    clients = (below, below + 1, member - 1)

    def u_copy(j):
        return remote(u_buf.at[clients[j]], prior_buf, send_u.at[j], recv_u, base + clients[j])

    def v_copy(j):
        return remote(u_buf.at[clients[j] + 1], end_buf, send_u.at[3 + j], recv_v, base + clients[j])

    def w_copy(j):
        return remote(mine_buf, mine_buf, send_w.at[j], recv_w, base + clients[j])

    def e_copy(i):
        other = (group + 1 + i // (LEADERS + 1)) * GROUP + GROUP - 1 - 2 * (i % (LEADERS + 1))
        return remote(own_buf, e_buf.at[group], send_e.at[i], recv_e.at[group], other)

    def own_copy(i):
        mate = GROUP - 1 - i
        mate = base + mate - jnp.where(mate <= member, 1, 0)
        return remote(own_buf, own_buf, send_own.at[i], recv_own, mate)

    def start_w():
        w_copy(2).start()

        @pl.when(serves)
        def _():
            w_copy(0).start()
            w_copy(1).start()

    def await_b(k):
        remote(b_out, b_buf.at[k], send_b.at[0], recv_b.at[k], me).wait_recv()

    def await_e(other):
        remote(e_buf.at[other], e_buf.at[other], send_e.at[0], recv_e.at[other], me).wait_recv()

    def relax_turn(k, state):
        await_b(k)
        (state,) = evolve(1, state)
        return plus(state, spread(b_buf[k]))

    def coarse_turn(other, before):
        await_e(other)
        (image,) = evolve(2, before)
        return plus(image, spread(e_buf[other]))

    def before_group(first):
        return lax.fori_loop(1, group, coarse_turn, first) if groups > 2 else first

    def serve(reached):
        reached = jnp.where(serves, reached, -1)

        @pl.when(reached == below)
        def _():
            u_copy(0).start()

        @pl.when(reached == below + 1)
        def _():
            u_copy(1).start()
            v_copy(0).start()

        @pl.when(reached == below + 2)
        def _():
            v_copy(1).start()

    def relax_pair(n, state):
        return relax_turn(2 * n + 1, relax_turn(2 * n, state))

    def replay_turn(k, state):
        state = relax_turn(k, state)
        u_buf[k + 1] = join(state)
        return state

    def replay_pair(n, state):
        return replay_turn(2 * n + 1, replay_turn(2 * n, state))

    def serving_turn(k, state):
        state = replay_turn(k, state)
        serve(k + 1)
        return state

    def pick(first, second):
        return tuple(jnp.where(opens, a, b) for a, b in zip(first, second))

    @pl.when(relaxes)
    def _():
        @pl.when(opens)
        def _():
            s_buf[...] = join(start)

        @pl.when(group > 0)
        def _():
            remote(r_out, s_buf, send_s, recv_s, me).wait_recv()

        group_start = spread(s_buf[...])
        (coarse_start,) = evolve(2, group_start)
        opening = pick(spread(zero_buf[1]), group_start)
        closing = lax.fori_loop(jnp.where(opens, 1, 0), 2, relax_pair, opening)
        for n in range(2, GROUP // 2):
            closing = relax_pair(n, closing)
        own_buf[...] = join(minus(closing, coarse_start))

        def start_e(i, carry):
            e_copy(i).start()
            return carry

        def start_own(i, carry):
            own_copy(i).start()
            return carry

        lax.fori_loop(0, listeners, start_e, 0)
        lax.fori_loop(0, GROUP - 1, start_own, 0)

    @pl.when(corrects)
    def _():
        (coarse_initial,) = evolve(2, start)
        await_e(0)
        earlier = before_group(plus(coarse_initial, spread(e_buf[0])))
        (state,), (image,) = evolve_all((1, (earlier,)), (2, (earlier,)))
        state = plus(state, spread(b_buf[0]))
        mine_buf[...] = join(image)
        for k in range(1, half - 1):
            (state,) = evolve(1, state)
            state = plus(state, spread(b_buf[k]))
            if k == half - 3:
                u_buf[half - 2] = join(state)
                u_copy(2).start()
                w_copy(2).start()
        u_buf[half - 1] = join(state)
        v_copy(2).start()
        tail_buf[0], tail_buf[1] = state

    @pl.when(leads)
    def _():
        (coarse_initial,) = evolve(2, start)

        @pl.when(group > 0)
        def _():
            await_b(0)
            await_b(1)
            await_e(0)

        earlier = before_group(pick(start, plus(coarse_initial, spread(e_buf[0]))))
        u_buf[0] = join(earlier)
        @pl.when(jnp.logical_and(serves, below == 0))
        def _():
            u_copy(0).start()


        (state,), (image,) = evolve_all((1, (earlier,)), (2, (earlier,)))
        state = pick(spread(zero_buf[0]), plus(state, spread(b_buf[0])))
        u_buf[1] = join(state)

        @pl.when(jnp.logical_and(serves, below == 0))
        def _():
            u_copy(1).start()
            v_copy(0).start()

        (state,) = evolve(1, state)
        state = pick(spread(zero_buf[1]), plus(state, spread(b_buf[1])))
        u_buf[2] = join(state)

        @pl.when(below <= 2)
        def _():
            serve(2)

        mine_buf[...] = join(image)

        @pl.when(below > 2)
        def _():
            start_w()

        state = lax.fori_loop(1, below // 2, replay_pair, state)

        @pl.when(below > 2)
        def _():
            serve(below)

        state = lax.fori_loop(jnp.maximum(below, 2), below + 2, serving_turn, state)
        @pl.when(below <= 2)
        def _():
            start_w()

        for i in range(GROUP // 4 - 1):
            state = replay_pair(below // 2 + 1 + i, state)
        u_copy(2).start()
        state = replay_turn(member - 1, state)
        tail_buf[0], tail_buf[1] = state
        v_copy(2).start()
        await_b(member)

    chains = jnp.logical_or(leads, corrects)
    follows = jnp.logical_not(chains)

    @pl.when(me >= 1)
    def _():
        remote(r_out, r_buf, send_r, recv_r, me).wait_recv()

    @pl.when(me >= 2)
    def _():
        remote(p_out, p_buf, send_p, recv_p, me).wait_recv()

    packed_ref[STEPS_DEV] = p_buf[...] - r_buf[...]

    @pl.when(follows)
    def _():
        remote(u_buf.at[0], prior_buf, send_u.at[0], recv_u, me).wait_recv()
        tail_buf[0], tail_buf[1] = spread(prior_buf[...])

    prior = tail_buf[0], tail_buf[1]
    (point,), (ending,) = evolve_all((0, (prior,)), (1, (prior,)))
    ending = join(ending) + b_buf[member]
    packed_ref[0] = join(point)
    for i in range(1, STEPS_DEV - 1):
        (point,) = evolve(0, point)
        packed_ref[i] = join(point)

    @pl.when(follows)
    def _():
        remote(u_buf.at[0], end_buf, send_u.at[0], recv_v, me).wait_recv()
        remote(mine_buf, mine_buf, send_w.at[0], recv_w, me).wait_recv()

    @pl.when(jnp.logical_not(relaxes))
    def _():
        remote(own_buf, own_buf, send_own.at[0], recv_own, me).wait_recv()

    @pl.when(chains)
    def _():
        end_buf[...] = ending

    ending = end_buf[...]
    mine = mine_buf[...] + own_buf[...]
    last = member == GROUP - 1
    packed_ref[STEPS_DEV - 1] = jnp.where(last, mine, ending)
    packed_ref[STEPS_DEV + 1] = mine
    packed_ref[STEPS_DEV + 2] = jnp.where(last, ending - mine, 0.0)
    over_relaxer(lambda copy: copy.wait_send())
    over_leaders(lambda copy: copy.wait_send(), jnp.logical_not(defers))

    @pl.when(me + 2 < devices)
    def _():
        p_copy.wait_send()

    @pl.when(me + 1 < devices)
    def _():
        r_copy.wait_send()

    def end_client(j):
        u_copy(j).wait_send()
        v_copy(j).wait_send()
        w_copy(j).wait_send()

    @pl.when(chains)
    def _():
        end_client(2)

    @pl.when(serves)
    def _():
        end_client(0)
        end_client(1)

    @pl.when(relaxes)
    def _():
        def end_e(i, carry):
            e_copy(i).wait_send()
            return carry

        def end_own(i, carry):
            own_copy(i).wait_send()
            return carry

        lax.fori_loop(0, listeners, end_e, 0)
        lax.fori_loop(0, GROUP - 1, end_own, 0)


def unpack(packed_ref, traj_ref, resid_ref, coarse_ref, defect_ref):
    cols = packed_ref.shape[2] // 2
    places = [(traj_ref, i) for i in range(STEPS_DEV)] + [(resid_ref, 0), (coarse_ref, 0), (defect_ref, 0)]
    for i, (ref, index) in enumerate(places):
        ref[index, 0] = packed_ref[i, :, :cols]
        ref[index, 1] = packed_ref[i, :, cols:]


assert 4 * LEADERS == GROUP


def shards(devices, initial, coarse_guess, feed_rate, kill_rate):
    rows, cols = initial.shape[1:]
    groups = devices // GROUP
    steps = (interval_time / STEPS_DEV, interval_time, interval_time * GROUP)
    tables = []
    for step in steps:
        tables += [jnp.asarray(table) for table in solve_tables(rows, cols, step)]
    state = (rows, 2 * cols)
    block = (1,) + initial.shape
    dma = pltpu.SemaphoreType.DMA
    whole = pl.BlockSpec(memory_space=pltpu.VMEM)
    remain = pl.BlockSpec(memory_space=pltpu.HBM)
    inputs = (initial, coarse_guess, feed_rate, kill_rate, *tables)
    buffer = pltpu.VMEM(state, jnp.float32)
    packed = pl.pallas_call(
        functools.partial(kernel, devices, (rows, cols)),
        out_shape=jax.ShapeDtypeStruct((PIECES,) + state, jnp.float32),
        in_specs=[remain] * INPUTS,
        out_specs=whole,
        scratch_shapes=[pltpu.VMEM(each.shape, each.dtype) for each in inputs]
        + [
            pltpu.VMEM((9,) + state, jnp.float32),
            pltpu.VMEM((GROUP,) + state, jnp.float32),
            buffer,
            buffer,
            buffer,
            pltpu.VMEM((groups,) + state, jnp.float32),
            pltpu.VMEM((GROUP + 1,) + state, jnp.float32),
        ]
        + [buffer] * 6
        + [pltpu.VMEM((2,) + state, jnp.float32), buffer, pltpu.VMEM((2,) + state, jnp.float32)]
        + [dma((LEADERS + 1,)), dma((GROUP,)), dma, dma]
        + [dma(((LEADERS + 1) * groups,)), dma((groups,)), dma((6,)), dma((3,))]
        + [dma] * 7
        + [dma((INPUTS,)), dma((GROUP - 1,)), dma],
        compiler_params=pltpu.CompilerParams(
            collective_id=0, has_side_effects=True, vmem_limit_bytes=VMEM_GRANT
        ),
    )(*[pltpu.with_memory_space_constraint(each, pltpu.HBM) for each in inputs])
    return pl.pallas_call(
        unpack,
        out_shape=[
            jax.ShapeDtypeStruct((STEPS_DEV,) + initial.shape, jnp.float32),
            jax.ShapeDtypeStruct(block, jnp.float32),
            jax.ShapeDtypeStruct(block, jnp.float32),
            jax.ShapeDtypeStruct(block, jnp.float32),
        ],
        in_specs=[whole],
        out_specs=[whole] * 4,
        compiler_params=pltpu.CompilerParams(vmem_limit_bytes=VMEM_GRANT),
    )(pltpu.with_memory_space_constraint(packed, pltpu.VMEM))


def solution(mesh):
    spread = P("tm", None, None, None)
    return jax.shard_map(
        functools.partial(shards, mesh.shape["tm"]),
        mesh=mesh,
        in_specs=(P(), spread, P(), P()),
        out_specs=(spread, spread, spread, spread),
        check_vma=False,
    )
```

profile of v0, /device:TPU:30, one launch (start us, length us, event | category | flops | bytes accessed | tf_op | source)
XLA Modules:
  0.0 21.4 jit_solution(17027368825184384294)
XLA Ops:
  0.6 19.9 %shard_map.129.packed_ref = f32[7,64,128]{2,1,0:T(8,128)S(1)} custom-call(f32[2,64,64]{2,1,0:T(8,128)} %refs_0_.1, f32[1,2,64,64]{3,2,1,0:T(8,128)} %refs_1_.1, f32[64,64]{1,0:T(8,128)} %refs_2_.1, f32[64,64]{1,0:T(8,128)} %refs_3_.1, bf16[2,192,256]{2,1,0:T(8,128)(2,1)} %constant.12.clone.refs_4_, bf16[2,64,256]{2,1,0:T(8,128)(2,1)} %constant.13.clone.refs_5_, ...), custom_call_target="tpu_custom_call" | custom-call | tf_op jit(solution)/shard_map/pallas_call | solution.py:653
  20.5 0.9 %shard_map.130 = (f32[4,2,64,64]{3,2,1,0:T(8,128)}, f32[1,2,64,64]{3,2,1,0:T(8,128)}, f32[1,2,64,64]{3,2,1,0:T(8,128)}, f32[1,2,64,64]{3,2,1,0:T(8,128)}) custom-call(f32[7,64,128]{2,1,0:T(8,128)S(1)} %shard_map.129.packed_ref), custom_call_target="tpu_custom_call" | custom-call | tf_op jit(solution)/shard_map/pallas_call | solution.py:678
where the time goes:
time: 21.5 us; the launch traced here: 21.4 us
  Pallas kernels  20.7 us (96%)
  between operations  0.64 us (3%)
    pallas_call x1, Pallas kernels, shards(): pl.pallas_call(functools.partial(kernel, devices, (rows, cols)), out_shap...  19.9 us
    pallas_call x1, Pallas kernels, shards(): pl.pallas_call(unpack, out_shape=[jax.ShapeDtypeStruct((STEPS_DEV,) + ini...  0.86 us

commit v1 on v0

--- a/solution.py
+++ b/solution.py
@@ -84,7 +84,7 @@
         highs = [high for high, low in pairs]
         lows = [low for high, low in pairs]
         if short:
-            lefts.append(np.concatenate(highs + highs[:1] + lows[:1], 1))
+            lefts.append(np.concatenate(highs[1:] + highs[:1] + lows[:1] + highs[:1], 1))
         else:
             lefts.append(np.concatenate(highs + highs + lows, 1))
     return np.stack(rights), np.stack(lefts)
@@ -229,7 +229,7 @@
             pieces = [part[rows * n : rows * (n + 1)] for part in parts]
             if terms == 2:
                 first_high, first_low = split(pieces[0])
-                stack = [first_high, pieces[1].astype(jnp.bfloat16), first_low, first_high]
+                stack = [pieces[1].astype(jnp.bfloat16), first_high, first_high, first_low]
             else:
                 pairs = [split(piece) for piece in pieces]
                 stack = [a for a, b in pairs] + [b for a, b in pairs] + [a for a, b in pairs]

time: 21.5 us -> 21.4 us (level)
  no operation moved by 1% of the time
where the time goes in v1:
time: 21.4 us; the launch traced here: 21.3 us
  Pallas kernels  20.6 us (96%)
  between operations  0.64 us (3%)
    pallas_call x1, Pallas kernels, shards(): pl.pallas_call(functools.partial(kernel, devices, (rows, cols)), out_shap...  19.8 us
    pallas_call x1, Pallas kernels, shards(): pl.pallas_call(unpack, out_shape=[jax.ShapeDtypeStruct((STEPS_DEV,) + ini...  0.86 us

profile of v1, /device:TPU:30, one launch (start us, length us, event | category | flops | bytes accessed | tf_op | source)
XLA Modules:
  0.0 21.3 jit_solution(17678901080694897105)
XLA Ops:
  0.6 19.8 %shard_map.129.packed_ref = f32[7,64,128]{2,1,0:T(8,128)S(1)} custom-call(f32[2,64,64]{2,1,0:T(8,128)} %refs_0_.1, f32[1,2,64,64]{3,2,1,0:T(8,128)} %refs_1_.1, f32[64,64]{1,0:T(8,128)} %refs_2_.1, f32[64,64]{1,0:T(8,128)} %refs_3_.1, bf16[2,192,256]{2,1,0:T(8,128)(2,1)} %constant.12.clone.refs_4_, bf16[2,64,256]{2,1,0:T(8,128)(2,1)} %constant.13.clone.refs_5_, ...), custom_call_target="tpu_custom_call" | custom-call | tf_op jit(solution)/shard_map/pallas_call | solution.py:653
  20.4 0.9 %shard_map.130 = (f32[4,2,64,64]{3,2,1,0:T(8,128)}, f32[1,2,64,64]{3,2,1,0:T(8,128)}, f32[1,2,64,64]{3,2,1,0:T(8,128)}, f32[1,2,64,64]{3,2,1,0:T(8,128)}) custom-call(f32[7,64,128]{2,1,0:T(8,128)S(1)} %shard_map.129.packed_ref), custom_call_target="tpu_custom_call" | custom-call | tf_op jit(solution)/shard_map/pallas_call | solution.py:678
